TPU v7x, 32 devices: a whole 2x2x4 slice. The times are simulated.
32 devices in a mesh: row: 2 (over y), col: 4 (over x, core), layer: 4 (over z).
Axes of the slice: x: 2, y: 2, z: 4, core: 2. Of those that a mesh axis runs over, the one named last changes fastest.
Arguments:
- left: float32 [1024, 8192], P('row', ('layer', 'col')), may hold values from -6 to 6
- right: float32 [8192, 16384], P(('layer', 'row'), 'col'), may hold values from -0.125 to 0.125
- left_mask: int32 [2, 16], replicated, may hold values 0 or 1
- right_mask: int32 [16, 32], replicated, may hold values 0 or 1
- result_mask: int32 [2, 32], replicated, may hold values 0 or 1
Outputs:
- ladder: float32 [1024, 16384], P('row', ('col', 'layer'))
Inputs may be any that keep to these rules, and one draw needn't show every extreme that they name: `left_mask`: 1 marks a present tile, 0 an absent one. `right_mask`: 1 marks a present tile, 0 an absent one. `result_mask`: 1 marks a present tile, 0 an absent one.
All inputs are finite; a program needn't handle non-finite values.
Results may differ from a plain program's by a relative error of at most 0.0003.
Values sent between devices are 32-bit elements; how exact they have to be, the bound alone decides.
A program may use at most 128 MiB of HBM per device.

v0:
```python
import jax
import jax.numpy as jnp
from jax import lax
from jax.sharding import PartitionSpec as P

TILE = 512


def expand(table, row_start, rows, col_start, cols):
    row_ids = (row_start + jnp.arange(rows, dtype=jnp.int32)) // TILE
    col_ids = (col_start + jnp.arange(cols, dtype=jnp.int32)) // TILE
    row_sel = (row_ids[:, None] == jnp.arange(table.shape[0], dtype=jnp.int32)[None, :]).astype(
        jnp.float32
    )
    col_sel = (col_ids[:, None] == jnp.arange(table.shape[1], dtype=jnp.int32)[None, :]).astype(
        jnp.float32
    )
    inner = jnp.dot(row_sel, table.astype(jnp.float32), precision=lax.Precision.HIGHEST)
    return jnp.dot(inner, col_sel.T, precision=lax.Precision.HIGHEST)


def shards(left, right, left_mask, right_mask, result_mask):
    rows, left_cols = left.shape
    right_rows, right_cols = right.shape
    row_pos = lax.axis_index("row")
    col_pos = lax.axis_index("col")
    layer_pos = lax.axis_index("layer")
    col_count = lax.axis_size("col")
    row_count = lax.axis_size("row")
    layer_count = lax.axis_size("layer")
    left_start = (layer_pos * col_count + col_pos) * left_cols
    right_start = (layer_pos * row_count + row_pos) * right_rows
    left_used = left * expand(left_mask, row_pos * rows, rows, left_start, left_cols)
    right_used = right * expand(
        right_mask, right_start, right_rows, col_pos * right_cols, right_cols
    )
    out_cols = right_cols // layer_count
    slab = lax.all_gather(right_used, "row", axis=0, tiled=True)
    partial_sum = jnp.dot(
        lax.all_gather(left_used, "col", axis=1, tiled=True),
        slab,
        precision=lax.Precision.HIGHEST,
        preferred_element_type=jnp.float32,
    )
    product = lax.psum_scatter(partial_sum, "layer", scatter_dimension=1, tiled=True)
    keep = expand(
        result_mask, row_pos * rows, rows, (col_pos * layer_count + layer_pos) * out_cols, out_cols
    )
    return product * keep


def solution(mesh):
    placed = (P("row", ("layer", "col")), P(("layer", "row"), "col"), P(), P(), P())
    return jax.shard_map(
        shards, mesh=mesh, in_specs=placed, out_specs=P("row", ("col", "layer")), check_vma=False
    )
```

profile of v0, /device:TPU:0, one launch (start us, length us, event | category | flops | bytes accessed | tf_op | source)
XLA Modules:
  0.0 652.3 jit_solution(17251776173520304404)
XLA Ops:
  6.5 0.0 all-gather.3.cloned.1.call-start
  6.6 1.0 fusion.5
  7.6 2.9 convolution_multiply_fusion.2
  10.5 0.0 all-gather.3.cloned.1.call-update
  10.5 0.0 all-gather.5.cloned.1.call-start
  10.6 1.2 fusion
  11.8 13.7 %convolution_multiply_fusion = f32[1024,4096]{1,0:T(8,128)} fusion(f32[1024,4096]{1,0:T(8,128)} %param.6, f32[1024,32]{1,0:T(8,128)S(1)} %fusion, s32[4096]{0:T(1024)S(1)} %add_select_fusion), kind=kOutput, calls=%fused_computation | convolution fusion | flops 1614938112 | bytes 33701888 | tf_op jit(solution)/shard_map/dot_general | solution.py:19
  25.4 0.0 all-gather.5.cloned.1.call-update
  25.4 0.0 reduce-scatter.2.cloned.1.call-start
  25.5 22.3 %all-gather.3.cloned.1.call-done = f32[512,2048]{1,0:T(8,128)} async-done(((f32[512,512]{1,0:T(8,128)}), f32[512,2048]{1,0:T(8,128)}) %all-gather.3.cloned.1.call-update) | async-done | bytes 4194320 | tf_op jit(solution)/shard_map/all_gather | solution.py:40
  47.8 390.1 %all-gather.5.cloned.1.call-done = f32[2048,4096]{1,0:T(8,128)} async-done(((f32[1024,4096]{1,0:T(8,128)}), f32[2048,4096]{1,0:T(8,128)}) %all-gather.5.cloned.1.call-update) | async-done | bytes 33554448 | tf_op jit(solution)/shard_map/all_gather | solution.py:38
  438.0 59.0 %fusion.27 = f32[512,4096]{1,0:T(8,128)} fusion(f32[512,2048]{1,0:T(8,128)} %all-gather.3.cloned.1.call-done, f32[2048,4096]{1,0:T(8,128)} %all-gather.5.cloned.1.call-done), kind=kOutput, calls=%fused_computation.65 | convolution fusion | flops 51539607552 | bytes 46137344 | tf_op jit(solution)/shard_map/dot_general | solution.py:39
  496.9 0.0 copy-start
  496.9 0.0 reduce-scatter.2.cloned.1.call-update
  497.0 0.6 copy-done
  497.6 0.3 fusion.4
  497.9 143.8 %reduce-scatter.2.cloned.1.call-done = f32[512,1024]{1,0:T(8,128)} async-done(((f32[512,4096]{1,0:T(8,128)}), f32[512,1024]{1,0:T(8,128)}) %reduce-scatter.2.cloned.1.call-update) | async-done | bytes 2097168 | tf_op jit(solution)/shard_map/reduce_scatter | solution.py:45
  641.7 4.0 convolution_multiply_fusion.1
  (5 shorter events, 0.1 us)
Async XLA Ops:
  6.5 41.3 %all-gather.3.cloned.1.call-start = ((), (), s32[]{:S(2)}) async-start(), calls=%async_computation.1 | async-start | bytes 5242880 | tf_op jit(solution)/shard_map/all_gather | solution.py:40
  10.5 427.5 %all-gather.5.cloned.1.call-start = ((), (), s32[]{:S(2)}) async-start(), calls=%async_computation.2 | async-start | bytes 50331648 | tf_op jit(solution)/shard_map/all_gather | solution.py:38
  25.4 616.3 %reduce-scatter.2.cloned.1.call-start = ((), (), s32[]{:S(2)}) async-start(), calls=%async_computation.3 | async-start | bytes 10485760 | tf_op jit(solution)/shard_map/reduce_scatter | solution.py:45
  496.9 0.7 copy-start
Sparse Core Ops, SparseCore 0:
  10.6 37.1 all-gather.2
  49.4 388.5 all-gather.4
  497.1 144.6 reduce-scatter.1
where the time goes:
time: 653 us; the launch traced here: 652 us
  waiting for transfers between devices  556 us (85%)
  matrix products  82 us (13%)
  between operations  13.2 us (2%)
    all_gather x1, waiting for transfers between devices, shards(): slab = lax.all_gather(right_used, 'row', axis=0, tiled=True)  390 us
    reduce_scatter x1, waiting for transfers between devices, shards(): lax.psum_scatter(partial_sum, 'layer', scatter_dimension=1, tiled=True)  144 us
    dot_general x1, matrix products, shards(): jnp.dot(lax.all_gather(left_used, 'col', axis=1, tiled=True), slab, preci...  59 us
    all_gather x1, waiting for transfers between devices, shards(): lax.all_gather(left_used, 'col', axis=1, tiled=True)  22.3 us
    dot_general x3, matrix products, expand(): return jnp.dot(inner, col_sel.T, precision=lax.Precision.HIGHEST)  20.5 us
  transfers between devices with their start and end apart: 3, of which 3 were waited for; matrix products, arithmetic and copies ran while one was open for 2% of the time, Pallas kernels for 0%

commit v1 on v0

--- a/solution.py
+++ b/solution.py
@@ -35,7 +35,15 @@
         right_mask, right_start, right_rows, col_pos * right_cols, right_cols
     )
     out_cols = right_cols // layer_count
-    slab = lax.all_gather(right_used, "row", axis=0, tiled=True)
+    ways, here = (lax.axis_size("row"), lax.axis_index("row"))
+    grown, reach = (right_used, 1)
+    while reach < ways:
+        theirs = lax.ppermute(grown, "row", [(d, d ^ reach) for d in range(ways)])
+        mine_first = jnp.concatenate([grown, theirs], axis=0)
+        theirs_first = jnp.concatenate([theirs, grown], axis=0)
+        grown = jnp.where(here & reach == 0, mine_first, theirs_first)
+        reach = 2 * reach
+    slab = grown
     partial_sum = jnp.dot(
         lax.all_gather(left_used, "col", axis=1, tiled=True),
         slab,

time: 653 us -> 603 us (0.923)
  waiting for transfers between devices: 556 us -> 503 us
    all_gather x1 -> x0, waiting for transfers between devices: 390 us -> none  [shards(): slab = lax.all_gather(right_used, 'row', axis=0, tiled=True)]
    ppermute x0 -> x1, waiting for transfers between devices: none -> 324 us  [shards(): theirs = lax.ppermute(grown, 'row', [(d, d ^ reach) for d in range(ways)])]
    all_gather x1, waiting for transfers between devices: 22.3 us -> 34.6 us  [shards(): lax.all_gather(left_used, 'col', axis=1, tiled=True)]
  transfers between devices with their start and end apart: 3 -> 3, of which waited for: 3 -> 3; matrix products, arithmetic and copies ran while one was open for 2% -> 1% of each run, Pallas kernels for 0% -> 0%
where the time goes in v1:
time: 603 us
  waiting for transfers between devices  503 us (83%)
  matrix products  79.4 us (13%)
  between operations  13.5 us (2%)
    ppermute x1, waiting for transfers between devices, shards(): theirs = lax.ppermute(grown, 'row', [(d, d ^ reach) for d in range(ways)])  324 us
    reduce_scatter x1, waiting for transfers between devices, shards(): lax.psum_scatter(partial_sum, 'layer', scatter_dimension=1, tiled=True)  145 us
    dot_general x1, matrix products, shards(): jnp.dot(lax.all_gather(left_used, 'col', axis=1, tiled=True), slab, preci...  61.4 us
    all_gather x1, waiting for transfers between devices, shards(): lax.all_gather(left_used, 'col', axis=1, tiled=True)  34.6 us
    dot_general x3, matrix products, expand(): return jnp.dot(inner, col_sel.T, precision=lax.Precision.HIGHEST)  16.3 us
  transfers between devices with their start and end apart: 3, of which 3 were waited for; matrix products, arithmetic and copies ran while one was open for 1% of the time, Pallas kernels for 0%

profile of v1, /device:TPU:0, one launch (start us, length us, event | category | flops | bytes accessed | tf_op | source)
XLA Modules:
  0.0 602.6 jit_solution(3392135930649259974)
XLA Ops:
  6.5 0.0 all-gather.2.cloned.1.call-start
  6.6 1.2 fusion.7
  7.7 0.0 copy-start.1
  7.8 0.0 copy-start
  7.8 13.5 %convolution_multiply_fusion = f32[1024,4096]{1,0:T(8,128)} fusion(f32[1024,4096]{1,0:T(8,128)} %param.6, f32[1024,32]{1,0:T(8,128)S(1)} %fusion.7, s32[4096]{0:T(1024)S(1)} %add_select_fusion), kind=kOutput, calls=%fused_computation.8 | convolution fusion | flops 1614938112 | bytes 33701888 | tf_op jit(solution)/shard_map/dot_general | solution.py:19
  21.3 3.0 collective-permute-start
  24.3 0.0 copy-done.1
  24.3 0.3 fusion.13
  24.7 0.0 copy-done
  24.7 1.7 convolution_multiply_fusion.1
  26.3 0.0 all-gather.2.cloned.1.call-update
  26.4 0.2 reduce-scatter.2.cloned.1.call-start
  26.6 0.0 copy-start.2
  26.6 34.6 %all-gather.2.cloned.1.call-done = f32[512,2048]{1,0:T(8,128)} async-done(((f32[512,512]{1,0:T(8,128)}), f32[512,2048]{1,0:T(8,128)}) %all-gather.2.cloned.1.call-update) | async-done | bytes 4194320 | tf_op jit(solution)/shard_map/all_gather | solution.py:48
  61.3 323.5 %collective-permute-done = f32[1024,4096]{1,0:T(8,128)} collective-permute-done((f32[1024,4096]{1,0:T(8,128)}, f32[1024,4096]{1,0:T(8,128)}, u32[]{:S(2)}, u32[]{:S(2)}) %collective-permute-start) | collective-permute-done | bytes 16777248 | tf_op jit(solution)/shard_map/ppermute | solution.py:41
  384.8 61.4 %fusion = f32[512,4096]{1,0:T(8,128)} fusion(f32[512,2048]{1,0:T(8,128)} %all-gather.2.cloned.1.call-done, f32[1024,4096]{1,0:T(8,128)} %collective-permute-done, f32[1024,4096]{1,0:T(8,128)} %convolution_multiply_fusion, pred[]{:T(512)S(6)} %eq.38), kind=kOutput, calls=%fused_computation.1 | convolution fusion | flops 51564773376 | bytes 46137344 | tf_op jit(solution)/shard_map/dot_general | solution.py:47
  446.2 0.0 reduce-scatter.2.cloned.1.call-update
  446.2 0.0 copy-done.2
  446.2 0.3 fusion.12
  446.6 1.1 fusion.8
  447.6 144.8 %reduce-scatter.2.cloned.1.call-done = f32[512,1024]{1,0:T(8,128)} async-done(((f32[512,4096]{1,0:T(8,128)}), f32[512,1024]{1,0:T(8,128)}) %reduce-scatter.2.cloned.1.call-update) | async-done | bytes 2097168 | tf_op jit(solution)/shard_map/reduce_scatter | solution.py:53
  592.4 3.3 mul.44
  (5 shorter events, 0.1 us)
Async XLA Ops:
  6.5 54.7 %all-gather.2.cloned.1.call-start = ((), (), s32[]{:S(2)}) async-start(), calls=%async_computation.1 | async-start | bytes 5242880 | tf_op jit(solution)/shard_map/all_gather | solution.py:48
  7.7 16.6 %copy-start.1 = (s32[2,16]{1,0:T(2,128)S(1)}, s32[2,16]{1,0:T(2,128)}, u32[]{:S(2)}) copy-start(s32[2,16]{1,0:T(2,128)} %param.7) | copy-start | bytes 388
  7.8 16.9 %copy-start = (f32[512,512]{1,0:T(8,128)S(1)}, f32[512,512]{1,0:T(8,128)}, u32[]{:S(2)}) copy-start(f32[512,512]{1,0:T(8,128)} %param.5) | copy-start | bytes 3145732
  21.3 363.5 %collective-permute-start = (f32[1024,4096]{1,0:T(8,128)}, f32[1024,4096]{1,0:T(8,128)}, u32[]{:S(2)}, u32[]{:S(2)}) collective-permute-start(f32[1024,4096]{1,0:T(8,128)} %convolution_multiply_fusion), channel_id=1, source_target_pairs={{0,16},{16,0},{1,17},{17,1},{2,18},{18,2},{3,19},{19,3},{4,20},{20... | collective-permute-start | bytes 50331656 | tf_op jit(solution)/shard_map/ppermute | solution.py:41
  26.4 566.1 %reduce-scatter.2.cloned.1.call-start = ((), (), s32[]{:S(2)}) async-start(), calls=%async_computation.2 | async-start | bytes 10485760 | tf_op jit(solution)/shard_map/reduce_scatter | solution.py:53
  26.6 419.6 %copy-start.2 = (s32[2,32]{1,0:T(2,128)S(1)}, s32[2,32]{1,0:T(2,128)}, u32[]{:S(2)}) copy-start(s32[2,32]{1,0:T(2,128)} %param.9) | copy-start | bytes 772
Sparse Core Ops, SparseCore 0:
  26.5 34.7 all-gather.1
  446.3 146.0 reduce-scatter.1
